TPU v7x, 256 devices: a whole 4x4x8 slice. The times are simulated.
256 devices in a mesh: seq: 32 (over x, y, core), head: 8 (over z).
Axes of the slice: x: 4, y: 4, z: 8, core: 2. Of those that a mesh axis runs over, the one named last changes fastest.
Arguments:
- queries: bfloat16 [24576, 8192], P('seq', 'head'), may hold values from -140 to 140
- key_weight: bfloat16 [1024, 8192], P(None, 'head'), may hold values from -0.1875 to 0.1875
- value_weight: bfloat16 [1024, 8192], P(None, 'head'), may hold values from -0.1875 to 0.1875
- encodings: bfloat16 [256, 128, 1024], P('seq', None, 'head'), may hold values from -6 to 6
- nb_owner: int32 [384, 2], P('seq'), may hold values from 0 to 31, all different within a row; in each aligned block of 12 rows (0 to 11, 12 to 23, ...) at most 2 rows name the same one
- nb_block: int32 [384, 2], P('seq'), may hold values from 0 to 7
Outputs:
- attended: bfloat16 [24576, 8192], P('seq', 'head')
Inputs may be any that keep to these rules, and one draw needn't show every extreme that they name: `nb_owner`: the 2 neighbours of a span have different owners. Among the spans of one device no owner is named more than 2 times, and in every draw some device names some owner exactly 2 times.
All inputs are finite; a program needn't handle non-finite values.
Results may differ from a plain program's by a relative error of at most 0.012.
The roundings to bfloat16 on the way count: a program that leaves them out, or rounds other values in their place, can miss the bound.
Values may be sent and summed in bfloat16 or wider, within the bound.
A program may use at most 128 MiB of HBM per device.

v0:
```python
import math

import jax
import jax.numpy as jnp
from jax import lax
from jax.sharding import PartitionSpec as P

HEAD_DIM = 128
SPAN = 64


def shifted(shard, axis, by):
    devices = lax.axis_size(axis)
    pairs = [(i, i + by) for i in range(devices) if 0 <= i + by < devices]
    return lax.ppermute(shard, axis, pairs)


def on_device(queries, key_weight, value_weight, encodings, nb_owner, nb_block):
    span_dev, neighbours = nb_owner.shape
    entries = span_dev * neighbours
    db_local, block_len, slice_width = encodings.shape
    group_width = key_weight.shape[1]
    group_heads = group_width // HEAD_DIM
    peer_count = lax.axis_size("seq")
    slot_most = max(2, (entries + peer_count - 1) // peer_count)
    owner_ids = nb_owner.reshape(entries)
    block_ids = nb_block.reshape(entries)
    position = jnp.arange(entries, dtype=jnp.int32)
    same_owner = owner_ids[:, None] == owner_ids[None, :]
    before = position[None, :] < position[:, None]
    slot_ids = jnp.sum((same_owner & before).astype(jnp.int32), axis=1)
    owner_hit = owner_ids[:, None] == jnp.arange(peer_count, dtype=jnp.int32)[None, :]
    slot_hit = slot_ids[:, None] == jnp.arange(slot_most, dtype=jnp.int32)[None, :]
    marked = owner_hit[:, :, None] & slot_hit[:, None, :]
    requests = jnp.sum(jnp.where(marked, (block_ids + 1)[:, None, None], 0), axis=0)
    asked_ids = lax.all_to_all(requests, "seq", split_axis=0, concat_axis=0, tiled=True)
    present = asked_ids > 0
    picked = jnp.take(encodings, jnp.maximum(asked_ids - 1, 0), axis=0)
    picked = jnp.where(present[:, :, None, None], picked, jnp.zeros_like(picked))
    replies = lax.all_to_all(picked, "seq", split_axis=0, concat_axis=0, tiled=True)
    slot_count = replies.shape[1]
    flat_rows = replies.reshape(peer_count * slot_count, block_len, slice_width)
    compact = jnp.take(flat_rows, owner_ids * slot_count + slot_ids, axis=0)
    full_width = lax.all_gather(compact, "head", axis=2, tiled=True)
    rows = full_width.reshape(-1, full_width.shape[2])
    key_rows = jnp.dot(rows, key_weight, preferred_element_type=jnp.float32).astype(jnp.bfloat16)
    value_rows = jnp.dot(rows, value_weight, preferred_element_type=jnp.float32).astype(
        jnp.bfloat16
    )
    key_rows, value_rows = (
        key_rows.reshape(span_dev, neighbours * block_len, group_heads, HEAD_DIM),
        value_rows.reshape(span_dev, neighbours * block_len, group_heads, HEAD_DIM),
    )
    stacked = jnp.stack([key_rows[span_dev - 1], value_rows[span_dev - 1]])
    earlier = shifted(stacked, "seq", 1)
    key_rows = jnp.concatenate([earlier[0][None], key_rows], axis=0)
    value_rows = jnp.concatenate([earlier[1][None], value_rows], axis=0)
    token_count = queries.shape[0]
    grouped = jnp.pad(queries, ((1, SPAN - 1), (0, 0))).reshape(
        span_dev + 1, SPAN, group_heads, HEAD_DIM
    )
    scores = jnp.einsum(
        "cqhd,ckhd->chqk", grouped, key_rows, preferred_element_type=jnp.float32
    ) * (1.0 / math.sqrt(HEAD_DIM))
    weights = jax.nn.softmax(scores, axis=-1).astype(jnp.bfloat16)
    attended = jnp.einsum(
        "chqk,ckhd->cqhd", weights, value_rows, preferred_element_type=jnp.float32
    )
    attended = attended.reshape((span_dev + 1) * SPAN, group_width)[1 : token_count + 1]
    return attended.astype(jnp.bfloat16)


def solution(mesh):
    return jax.shard_map(
        on_device,
        mesh=mesh,
        in_specs=(
            P("seq", "head"),
            P(None, "head"),
            P(None, "head"),
            P("seq", None, "head"),
            P("seq", None),
            P("seq", None),
        ),
        out_specs=P("seq", "head"),
        check_vma=False,
    )
```

profile of v0, /device:TPU:1, one launch (start us, length us, event | category | flops | bytes accessed | tf_op | source)
XLA Modules:
  0.0 267.6 jit_solution(14205049635166241465)
XLA Ops:
  6.5 0.9 copy.63
  7.5 0.1 reshape.149
  7.5 0.2 convert_reduce_fusion
  7.7 0.1 iota_compare_fusion
  7.8 0.7 broadcast_add_fusion
  8.5 0.1 copy.64
  8.6 0.1 add.60
  8.7 0.1 select_reduce_fusion
  8.8 0.1 copy.65
  8.9 15.3 %all_to_all.14 = s32[32,1,2]{2,1,0:T(1,128)S(1)} all-to-all(s32[32,1,2]{2,1,0:T(1,128)S(1)} %copy.65), channel_id=1, replica_groups=mesh['seq'=32,'head'=8] {'seq'}, dimensions={0} | all-to-all | bytes 512 | tf_op jit(solution)/shard_map/all_to_all | solution.py:36
  24.2 0.1 copy.66
  24.3 0.1 copy.67
  24.4 0.1 copy.69
  24.5 0.1 copy.70
  24.6 0.1 reshape.158
  24.7 3.1 %gather_fusion = bf16[64,128,128]{2,1,0:T(8,128)(2,1)} fusion(bf16[8,128,128]{2,1,0:T(8,128)(2,1)} %param.9, s32[1024]{0:T(1024)S(1)} %pad_clamp_fusion.1), kind=kCustom, calls=%fused_computation | custom fusion | bytes 4194560 | tf_op jit(solution)/shard_map/jit(_take)/gather | solution.py:38
  27.8 3.3 %select_select_fusion = bf16[32,2,128,128]{3,2,1,0:T(8,128)(2,1)} fusion(bf16[32,2,128,128]{3,2,1,0:T(8,128)(2,1)} %bitcast.37, pred[32,2]{1,0:T(8,128)(4,1)S(1)} %copy.69, pred[32,2]{1,0:T(8,128)(4,1)S(1)} %copy.67), kind=kLoop, calls=%fused_computation.19 | loop fusion | flops 2097152 | bytes 4194432 | tf_op jit(solution)/shard_map/jit(_where)/select_n | solution.py:39
  31.1 5.0 %all-to-all-start.1 = ((bf16[32,2,128,128]{3,2,1,0:T(8,128)(2,1)}), bf16[32,2,128,128]{3,2,1,0:T(8,128)(2,1)}, u32[]{:S(2)}, u32[]{:S(2)}) async-start(bf16[32,2,128,128]{3,2,1,0:T(8,128)(2,1)} %select_select_fusion), calls=%async_computation.1 | async-start | bytes 4194304 | tf_op jit(solution)/shard_map/all_to_all | solution.py:40
  36.1 0.1 copy.71
  36.2 0.1 mul.25
  36.4 28.2 %all-to-all-done.1 = bf16[32,2,128,128]{3,2,1,0:T(8,128)(2,1)} async-done(((bf16[32,2,128,128]{3,2,1,0:T(8,128)(2,1)}), bf16[32,2,128,128]{3,2,1,0:T(8,128)(2,1)}, u32[]{:S(2)}, u32[]{:S(2)}) %all-to-all-start.1) | async-done | bytes 2097184 | tf_op jit(solution)/shard_map/all_to_all | solution.py:40
  64.5 2.3 gather_fusion.1
  66.8 1.0 broadcast_select_fusion
  67.9 75.7 %all-gather.2.cloned.1.call-done = bf16[24,128,1024]{2,1,0:T(8,128)(2,1)} async-done(((bf16[24,128,128]{2,1,0:T(8,128)(2,1)}), bf16[24,128,1024]{2,1,0:T(8,128)(2,1)}) %all-gather.2.cloned.1.call-update) | async-done | bytes 6291472 | tf_op jit(solution)/shard_map/all_gather | solution.py:44
  143.6 9.8 %convolution_convert_fusion.1 = bf16[3072,1024]{0,1:T(8,128)(2,1)S(1)} fusion(bf16[3072,1024]{1,0:T(8,128)(2,1)} %bitcast.44, bf16[1024,1024]{1,0:T(8,128)(2,1)S(1)} %copy-done), kind=kOutput, calls=%fused_computation.16 | convolution fusion | flops 6445596672 | bytes 14680064 | tf_op jit(solution)/shard_map/dot_general | solution.py:46
  153.4 2.6 copy-done.2
  156.0 0.1 slice.33
  156.1 0.3 copy.72
  156.4 9.5 %convolution_convert_fusion = bf16[3072,1024]{0,1:T(8,128)(2,1)S(1)} fusion(bf16[3072,1024]{1,0:T(8,128)(2,1)} %bitcast.45, bf16[1024,1024]{1,0:T(8,128)(2,1)} %param.8), kind=kOutput, calls=%fused_computation.15 | convolution fusion | flops 6445596672 | bytes 14680064 | tf_op jit(solution)/shard_map/dot_general | solution.py:47
  165.9 2.6 copy-done.3
  168.5 0.1 slice.34
  168.6 0.3 copy.73
  168.9 1.1 pad_maximum_fusion
  170.0 6.6 %collective-permute-start = (bf16[2,256,8,128]{3,1,2,0:T(8,128)(2,1)}, bf16[2,256,8,128]{3,1,2,0:T(8,128)(2,1)S(1)}, u32[]{:S(2)}, u32[]{:S(2)}) collective-permute-start(bf16[2,256,8,128]{3,1,2,0:T(8,128)(2,1)} %pad_maximum_fusion), channel_id=1, source_target_pairs={{0,8},{8,16},{16,24},{24,32},{32,40},{40,48},{48,56},{56,64},{64,7... | collective-permute-start | bytes 3145736 | tf_op jit(solution)/shard_map/ppermute | solution.py:15
  176.6 1.9 pad_bitcast_fusion
  178.5 1.7 copy.84
  180.2 12.0 %reshape.175 = bf16[12,256,8,128]{1,0,3,2:T(8,128)(2,1)} reshape(bf16[3072,1024]{0,1:T(8,128)(2,1)} %copy-done.2) | data formatting | bytes 12582912 | tf_op jit(solution)/shard_map/reshape | solution.py:51
  192.2 12.0 %reshape.174 = bf16[12,256,8,128]{1,0,3,2:T(8,128)(2,1)} reshape(bf16[3072,1024]{0,1:T(8,128)(2,1)} %copy-done.3) | data formatting | bytes 12582912 | tf_op jit(solution)/shard_map/reshape | solution.py:52
  204.3 11.9 %copy.77 = bf16[12,256,8,128]{3,1,2,0:T(8,128)(2,1)} copy(bf16[12,256,8,128]{1,0,3,2:T(8,128)(2,1)} %reshape.175) | data formatting | bytes 12582912 | tf_op jit(solution)/shard_map/reshape | solution.py:51
  216.2 12.1 %copy.75 = bf16[12,256,8,128]{3,1,2,0:T(8,128)(2,1)} copy(bf16[12,256,8,128]{1,0,3,2:T(8,128)(2,1)} %reshape.174) | data formatting | bytes 12582912 | tf_op jit(solution)/shard_map/reshape | solution.py:52
  228.3 0.9 fusion.33
  229.1 4.5 %fusion.1 = f32[13,8,64,256]{3,2,1,0:T(8,128)S(1)} fusion(bf16[12,256,8,128]{3,1,2,0:T(8,128)(2,1)} %copy.77, bf16[1,256,8,128]{3,1,2,0:T(8,128)(2,1)S(1)} %get-tuple-element.5, bf16[13,64,8,128]{3,2,1,0:T(8,128)(2,1)S(1)} %bitcast.39), kind=kOutput, calls=%fused_computation.3 | convolution fusion | flops 439615488 | bytes 15335424 | tf_op jit(solution)/shard_map/cqhd,ckhd->chqk/dot_general | solution.py:62
  233.7 2.8 %copy-done.4 = f32[13,8,64,256]{3,2,1,0:T(8,128)} copy-done((f32[13,8,64,256]{3,2,1,0:T(8,128)}, f32[13,8,64,256]{3,2,1,0:T(8,128)S(1)}, u32[]{:S(2)}) %copy-start.4) | copy-done | bytes 6815768
  236.4 2.6 fusion.34
  239.0 16.8 %fusion.18 = bf16[13,64,8,128]{3,1,2,0:T(8,128)(2,1)} fusion(bf16[12,256,8,128]{3,1,2,0:T(8,128)(2,1)} %copy.75, bf16[1,256,8,128]{3,1,2,0:T(8,128)(2,1)S(1)} %copy-done.6, f32[13,8,64]{2,1,0:T(8,128)S(1)} %fusion.34, f32[13,8,64,256]{3,2,1,0:T(8,128)} %copy-done.4), kind=kOutput, calls=%fused_computation.24 | convolution fusion | flops 459217664 | bytes 15362048 | tf_op jit(solution)/shard_map/chqk,ckhd->cqhd/dot_general | solution.py:66
  255.8 2.8 %copy.79 = bf16[13,64,8,128]{3,2,1,0:T(8,128)(2,1)S(1)} copy(bf16[13,64,8,128]{3,1,2,0:T(8,128)(2,1)} %fusion.18) | data formatting | bytes 3407872 | tf_op jit(solution)/shard_map/chqk,ckhd->cqhd/transpose | solution.py:66
  258.6 0.5 copy.89
  259.1 1.6 slice.37
  (24 shorter events, 0.1 us)
Async XLA Ops:
  6.5 137.0 %copy-start = (bf16[1024,1024]{1,0:T(8,128)(2,1)S(1)}, bf16[1024,1024]{1,0:T(8,128)(2,1)}, u32[]{:S(2)}) copy-start(bf16[1024,1024]{1,0:T(8,128)(2,1)} %param.7) | copy-start | bytes 6291460
  24.7 11.4 %copy-start.7 = (s32[12,2]{0,1:T(2,128)S(1)}, s32[12,2]{0,1:T(2,128)}, u32[]{:S(2)}) copy-start(s32[12,2]{0,1:T(2,128)} %param.10) | copy-start | bytes 292
  31.1 33.5 %all-to-all-start.1 = ((bf16[32,2,128,128]{3,2,1,0:T(8,128)(2,1)}), bf16[32,2,128,128]{3,2,1,0:T(8,128)(2,1)}, u32[]{:S(2)}, u32[]{:S(2)}) async-start(bf16[32,2,128,128]{3,2,1,0:T(8,128)(2,1)} %select_select_fusion), calls=%async_computation.1 | async-start | bytes 4194304 | tf_op jit(solution)/shard_map/all_to_all | solution.py:40
  36.1 107.5 %all-gather.2.cloned.1.call-start = ((), (), s32[]{:S(2)}) async-start(), calls=%async_computation.2 | async-start | bytes 7077888 | tf_op jit(solution)/shard_map/all_gather | solution.py:44
  153.4 2.7 copy-start.2
  165.9 2.6 copy-start.3
  170.0 58.3 %collective-permute-start = (bf16[2,256,8,128]{3,1,2,0:T(8,128)(2,1)}, bf16[2,256,8,128]{3,1,2,0:T(8,128)(2,1)S(1)}, u32[]{:S(2)}, u32[]{:S(2)}) collective-permute-start(bf16[2,256,8,128]{3,1,2,0:T(8,128)(2,1)} %pad_maximum_fusion), channel_id=1, source_target_pairs={{0,8},{8,16},{16,24},{24,32},{32,40},{40,48},{48,56},{56,64},{64,7... | collective-permute-start | bytes 3145736 | tf_op jit(solution)/shard_map/ppermute | solution.py:15
  216.2 13.0 %copy-start.5 = (bf16[104,8,8,128]{3,2,1,0:T(8,128)(2,1)S(1)}, bf16[104,8,8,128]{3,2,1,0:T(8,128)(2,1)}, u32[]{:S(2)}) copy-start(bf16[104,8,8,128]{3,2,1,0:T(8,128)(2,1)} %copy.84) | copy-start | bytes 5111812
  233.6 2.8 %copy-start.4 = (f32[13,8,64,256]{3,2,1,0:T(8,128)}, f32[13,8,64,256]{3,2,1,0:T(8,128)S(1)}, u32[]{:S(2)}) copy-start(f32[13,8,64,256]{3,2,1,0:T(8,128)S(1)} %fusion.1) | copy-start | bytes 20447236
  236.4 2.6 copy-start.6
  239.0 21.7 %copy-start.1 = (bf16[1024,1024]{1,0:T(8,128)(2,1)S(1)}, bf16[1024,1024]{1,0:T(8,128)(2,1)}, u32[]{:S(2)}) copy-start(bf16[1024,1024]{1,0:T(8,128)(2,1)} %param.7) | copy-start | bytes 6291460
Sparse Core Ops, SparseCore 0:
  68.0 75.5 all-gather.1
where the time goes:
time: 269 us; the launch traced here: 268 us
  waiting for transfers between devices  104 us (39%)
  local copies, waits for them, and re-layouts  73.5 us (27%)
  matrix products  40.6 us (15%)
  blocking collectives  15.3 us (6%)
  between operations  13.6 us (5%)
  starting transfers between devices  11.6 us (4%)
  other arithmetic  9.01 us (3%)
    all_gather x1, waiting for transfers between devices, on_device(): full_width = lax.all_gather(compact, 'head', axis=2, tiled=True)  75.7 us
    all_to_all x1, waiting for transfers between devices, on_device(): lax.all_to_all(picked, 'seq', split_axis=0, concat_axis=0, tiled=True)  28.2 us
    reshape x2, local copies, waits for them, and re-layouts, on_device(): value_rows.reshape(span_dev, neighbours * block_len, group_heads, HEAD_DIM)  24.1 us
    reshape x2, local copies, waits for them, and re-layouts, on_device(): key_rows.reshape(span_dev, neighbours * block_len, group_heads, HEAD_DIM)  23.9 us
    dot_general x1, matrix products, on_device(): jnp.einsum('chqk,ckhd->cqhd', weights, value_rows, preferred_element_type...  16.8 us
    all_to_all x1, blocking collectives, on_device(): lax.all_to_all(requests, 'seq', split_axis=0, concat_axis=0, tiled=True)  15.3 us
    unnamed x20, local copies, waits for them, and re-layouts  13.1 us
    dot_general x1, matrix products, on_device(): jnp.dot(rows, key_weight, preferred_element_type=jnp.float32)  9.79 us
  transfers between devices with their start and end apart: 3, of which 2 were waited for; matrix products, arithmetic and copies ran while one was open for 19% of the time, Pallas kernels for 0%

commit v1 on v0

v1 whole, which is shorter than its diff:
```python
import math

import jax
import jax.numpy as jnp
from jax import lax
from jax.experimental import pallas as pl
from jax.experimental.pallas import tpu as pltpu
from jax.sharding import PartitionSpec as P

HEAD_DIM = 128
SPAN = 64
CHUNK_SPANS = 2


def moved(shard, axis, by):
    devices = lax.axis_size(axis)
    pairs = [(i, i + by) for i in range(devices) if 0 <= i + by < devices]
    return lax.ppermute(shard, axis, pairs)


def project(x, wk_ref, wv_ref, kv):
    width = wk_ref.shape[1]
    for base, w_ref in ((0, wk_ref), (width, wv_ref)):

        @pl.loop(0, width // 256)
        def _(n):
            src = pl.ds(pl.multiple_of(n * 256, 256), 256)
            dst = pl.ds(pl.multiple_of(base + n * 256, 256), 256)
            kv[:, dst] = jnp.dot(
                x[...], w_ref[:, src], preferred_element_type=jnp.float32
            ).astype(jnp.bfloat16)


def attend(q_ref, q_start, kv, k_start, window, width, o_ref):
    rows = pl.ds(q_start, SPAN)
    keys = pl.ds(k_start, window)
    for h in range(width // HEAD_DIM):
        cols = slice(h * HEAD_DIM, (h + 1) * HEAD_DIM)
        vcols = slice(width + h * HEAD_DIM, width + (h + 1) * HEAD_DIM)
        s = lax.dot_general(
            q_ref[rows, cols],
            kv[keys, cols],
            (((1,), (1,)), ((), ())),
            preferred_element_type=jnp.float32,
        ) * (1.0 / math.sqrt(HEAD_DIM))
        e = jnp.exp(s - jnp.max(s, axis=-1, keepdims=True))
        w = (e * (1.0 / jnp.sum(e, axis=-1, keepdims=True))).astype(jnp.bfloat16)
        o_ref[rows, cols] = jnp.dot(
            w, kv[keys, vcols], preferred_element_type=jnp.float32
        ).astype(jnp.bfloat16)


def compute_kernel(g_ref, wk_ref, wv_ref, q_ref, o_ref, xs, kv):
    slices, rows, part = g_ref.shape
    width = wk_ref.shape[1]
    chunk_rows = xs.shape[0]
    window = chunk_rows // CHUNK_SPANS

    @pl.loop(0, rows // chunk_rows)
    def _(c):
        start = pl.multiple_of(c * chunk_rows, chunk_rows)
        for f in range(slices):
            xs[:, f * part : (f + 1) * part] = g_ref[f, pl.ds(start, chunk_rows), :]
        project(xs, wk_ref, wv_ref, kv)
        for j in range(CHUNK_SPANS):
            q_start = pl.multiple_of((c * CHUNK_SPANS + j) * SPAN, SPAN)
            attend(q_ref, q_start, kv, j * window, window, width, o_ref)


def fetch_blocks(encodings, nb_owner, nb_block):
    span_dev, neighbours = nb_owner.shape
    entries = span_dev * neighbours
    db_local, block_len, slice_width = encodings.shape
    peer_count = lax.axis_size("seq")
    slot_most = max(2, (entries + peer_count - 1) // peer_count)
    owner_ids = nb_owner.reshape(entries)
    block_ids = nb_block.reshape(entries)
    position = jnp.arange(entries, dtype=jnp.int32)
    same_owner = owner_ids[:, None] == owner_ids[None, :]
    before = position[None, :] < position[:, None]
    slot_ids = jnp.sum((same_owner & before).astype(jnp.int32), axis=1)
    owner_hit = owner_ids[:, None] == jnp.arange(peer_count, dtype=jnp.int32)[None, :]
    slot_hit = slot_ids[:, None] == jnp.arange(slot_most, dtype=jnp.int32)[None, :]
    marked = owner_hit[:, :, None] & slot_hit[:, None, :]
    requests = jnp.sum(jnp.where(marked, block_ids[:, None, None], 0), axis=0)
    asked_ids = lax.all_to_all(requests, "seq", split_axis=0, concat_axis=0, tiled=True)
    picked = jnp.take(encodings, asked_ids, axis=0)
    replies = lax.all_to_all(picked, "seq", split_axis=0, concat_axis=0, tiled=True)
    flat_rows = replies.reshape(peer_count * slot_most, block_len, slice_width)
    return jnp.take(flat_rows, owner_ids * slot_most + slot_ids, axis=0)


def on_device(queries, key_weight, value_weight, encodings, nb_owner, nb_block):
    span_dev, neighbours = nb_owner.shape
    token_count, width = queries.shape
    block_len, part = encodings.shape[1:]
    early = SPAN - 1
    ahead = moved(queries[:early], "seq", -1)
    lined = jnp.concatenate([queries[early:], ahead], axis=0)
    compact = fetch_blocks(encodings, nb_owner, nb_block)
    gathered = lax.all_gather(compact, "head", axis=0, tiled=False)
    gathered = gathered.reshape(gathered.shape[0], -1, part)
    chunk_rows = CHUNK_SPANS * neighbours * block_len
    vmem = pl.BlockSpec(memory_space=pltpu.VMEM)
    made = pl.pallas_call(
        compute_kernel,
        out_shape=jax.ShapeDtypeStruct((token_count, width), jnp.bfloat16),
        in_specs=[vmem] * 4,
        out_specs=vmem,
        scratch_shapes=[
            pltpu.VMEM((chunk_rows, gathered.shape[0] * part), jnp.bfloat16),
            pltpu.VMEM((chunk_rows, 2 * width), jnp.bfloat16),
        ],
        compiler_params=pltpu.CompilerParams(vmem_limit_bytes=48 << 20),
    )(gathered, key_weight, value_weight, lined)
    back = moved(made[token_count - early :], "seq", 1)
    return jnp.concatenate([back, made[: token_count - early]], axis=0)


def solution(mesh):
    return jax.shard_map(
        on_device,
        mesh=mesh,
        in_specs=(
            P("seq", "head"),
            P(None, "head"),
            P(None, "head"),
            P("seq", None, "head"),
            P("seq", None),
            P("seq", None),
        ),
        out_specs=P("seq", "head"),
        check_vma=False,
    )
```

time: 269 us -> 212 us (0.79)
  local copies, waits for them, and re-layouts: 73.5 us -> 6.78 us
  Pallas kernels: 0 us -> 58.5 us
  matrix products: 40.6 us -> 0 us
  waiting for transfers between devices: 104 us -> 99.4 us
  other arithmetic: 9.01 us -> 4.73 us
    pallas_call x0 -> x1, Pallas kernels: none -> 58.5 us  [on_device(): pl.pallas_call(compute_kernel, out_shape=jax.ShapeDtypeStruct((token_coun...]
    reshape x5 -> x1, local copies, waits for them, and re-layouts: 48.2 us -> 0.08 us  [fetch_blocks(): owner_ids = nb_owner.reshape(entries)]
    dot_general x4 -> x0, matrix products: 40.6 us -> none  [the longest x1 16.8 us: on_device(): jnp.einsum('chqk,ckhd->cqhd', weights, value_rows, preferred_element_type...]
    all_gather x1, waiting for transfers between devices: 75.7 us -> 66.3 us  [on_device(): gathered = lax.all_gather(compact, 'head', axis=0, tiled=False)]
    unnamed x20 -> x10, local copies, waits for them, and re-layouts: 13.1 us -> 3.83 us
    ppermute x1 -> x2, waiting for transfers between devices: 0.01 us -> 5.01 us  [moved(): return lax.ppermute(shard, axis, pairs)]
    gather x2, local copies, waits for them, and re-layouts: 5.36 us -> 1.65 us  [the longest x1 0.95 us: fetch_blocks(): picked = jnp.take(encodings, asked_ids, axis=0)]
    transpose x1 -> x0, local copies, waits for them, and re-layouts: 2.82 us -> none  [on_device(): jnp.einsum('chqk,ckhd->cqhd', weights, value_rows, preferred_element_type...]
  transfers between devices with their start and end apart: 3 -> 4, of which waited for: 2 -> 4; matrix products, arithmetic and copies ran while one was open for 19% -> 0% of each run, Pallas kernels for 0% -> 0%
where the time goes in v1:
time: 212 us; the launch traced here: 209 us
  waiting for transfers between devices  99.4 us (47%)
  Pallas kernels  58.5 us (28%)
  blocking collectives  15.3 us (7%)
  between operations  13.6 us (6%)
  starting transfers between devices  11.1 us (5%)
  local copies, waits for them, and re-layouts  6.78 us (3%)
  other arithmetic  4.73 us (2%)
    all_gather x1, waiting for transfers between devices, on_device(): gathered = lax.all_gather(compact, 'head', axis=0, tiled=False)  66.3 us
    pallas_call x1, Pallas kernels, on_device(): pl.pallas_call(compute_kernel, out_shape=jax.ShapeDtypeStruct((token_coun...  58.5 us
    all_to_all x1, waiting for transfers between devices, fetch_blocks(): lax.all_to_all(picked, 'seq', split_axis=0, concat_axis=0, tiled=True)  28.1 us
    all_to_all x1, blocking collectives, fetch_blocks(): lax.all_to_all(requests, 'seq', split_axis=0, concat_axis=0, tiled=True)  15.3 us
    ppermute x2, starting transfers between devices, moved(): return lax.ppermute(shard, axis, pairs)  6.57 us
    ppermute x2, waiting for transfers between devices, moved(): return lax.ppermute(shard, axis, pairs)  5.01 us
    all_to_all x1, starting transfers between devices, fetch_blocks(): lax.all_to_all(picked, 'seq', split_axis=0, concat_axis=0, tiled=True)  4.45 us
  transfers between devices with their start and end apart: 4, of which 4 were waited for; matrix products, arithmetic and copies ran while one was open for 0% of the time, Pallas kernels for 0%

profile of v1, /device:TPU:1, one launch (start us, length us, event | category | flops | bytes accessed | tf_op | source)
XLA Modules:
  0.0 209.4 jit_solution(11239079321875247384)
XLA Ops:
  6.5 0.0 copy-start
  6.5 0.8 copy.25
  7.3 0.1 reshape.130
  7.4 0.2 convert_reduce_fusion
  7.6 0.1 iota_compare_fusion
  7.7 0.8 copy.26
  8.5 0.1 broadcast_in_dim.42
  8.6 0.1 select_reduce_fusion
  8.7 0.1 copy.27
  8.7 15.3 %all_to_all.20 = s32[32,1,2]{2,1,0:T(1,128)S(1)} all-to-all(s32[32,1,2]{2,1,0:T(1,128)S(1)} %copy.27), channel_id=1, replica_groups=mesh['seq'=32,'head'=8] {'seq'}, dimensions={0} | all-to-all | bytes 512 | tf_op jit(solution)/shard_map/all_to_all | solution.py:86
  24.1 0.1 copy.28
  24.2 0.1 copy.29
  24.3 0.1 copy.31
  24.4 0.1 reshape.135
  24.5 0.0 copy-done
  24.5 1.0 gather_fusion
  25.5 1.6 broadcast_select_fusion
  27.1 0.0 copy-start.3
  27.1 4.5 %all-to-all-start.1 = ((bf16[32,2,128,128]{3,2,1,0:T(8,128)(2,1)}), bf16[32,2,128,128]{3,2,1,0:T(8,128)(2,1)S(1)}, u32[]{:S(2)}, u32[]{:S(2)}) async-start(bf16[32,2,128,128]{3,2,1,0:T(8,128)(2,1)} %broadcast_select_fusion), calls=%async_computation.1 | async-start | bytes 4194304 | tf_op jit(solution)/shard_map/all_to_all | solution.py:88
  31.5 0.0 all-gather.2.cloned.1.call-start
  31.6 0.0 copy-done.3
  31.6 0.1 copy.32
  31.7 0.1 mul.19
  31.8 28.1 %all-to-all-done.1 = bf16[32,2,128,128]{3,2,1,0:T(8,128)(2,1)S(1)} async-done(((bf16[32,2,128,128]{3,2,1,0:T(8,128)(2,1)}), bf16[32,2,128,128]{3,2,1,0:T(8,128)(2,1)S(1)}, u32[]{:S(2)}, u32[]{:S(2)}) %all-to-all-start.1) | async-done | bytes 2097184 | tf_op jit(solution)/shard_map/all_to_all | solution.py:88
  60.0 0.7 gather_fusion.1
  60.7 0.0 copy-start.2
  60.7 1.0 bitcast_select_fusion
  61.7 0.0 all-gather.2.cloned.1.call-update
  61.7 0.6 copy-done.2
  62.4 2.7 %collective-permute-start = (bf16[63,1024]{1,0:T(8,128)(2,1)S(1)}, bf16[63,1024]{1,0:T(8,128)(2,1)S(1)}, u32[]{:S(2)}, u32[]{:S(2)}) collective-permute-start(bf16[63,1024]{1,0:T(8,128)(2,1)S(1)} %slice.13), channel_id=1, source_target_pairs={{8,0},{16,8},{24,16},{32,24},{40,32},{48,40},{56,48},{64,56},{72,6... | collective-permute-start | bytes 387080 | tf_op jit(solution)/shard_map/ppermute | solution.py:18
  65.1 0.3 slice.12
  65.5 3.2 %collective-permute-done = bf16[63,1024]{1,0:T(8,128)(2,1)S(1)} collective-permute-done((bf16[63,1024]{1,0:T(8,128)(2,1)S(1)}, bf16[63,1024]{1,0:T(8,128)(2,1)S(1)}, u32[]{:S(2)}, u32[]{:S(2)}) %collective-permute-start) | collective-permute-done | bytes 129056 | tf_op jit(solution)/shard_map/ppermute | solution.py:18
  68.7 0.2 pad_maximum_fusion.q_ref
  68.8 66.3 %all-gather.2.cloned.1.call-done = bf16[8,24,128,128]{3,2,1,0:T(8,128)(2,1)} async-done(((bf16[1,24,128,128]{3,2,1,0:T(8,128)(2,1)}), bf16[8,24,128,128]{3,2,1,0:T(8,128)(2,1)}) %all-gather.2.cloned.1.call-update) | async-done | bytes 6291472 | tf_op jit(solution)/shard_map/all_gather | solution.py:101
  135.1 0.0 copy-start.1
  135.1 1.6 copy-done.1
  136.7 58.5 %shard_map.64 = bf16[768,1024]{1,0:T(8,128)(2,1)S(1)} custom-call(bf16[8,3072,128]{2,1,0:T(8,128)(2,1)} %bitcast.19, bf16[1024,1024]{1,0:T(8,128)(2,1)S(1)} %copy-done.1, bf16[1024,1024]{1,0:T(8,128)(2,1)} %wv_ref.1, bf16[768,1024]{1,0:T(8,128)(2,1)S(1)} %pad_maximum_fusion.q_ref), custom_call_target="tpu_custom_call" | custom-call | tf_op jit(solution)/shard_map/pallas_call | solution.py:105
  195.2 3.8 %collective-permute-start.1 = (bf16[63,1024]{1,0:T(8,128)(2,1)S(1)}, bf16[63,1024]{1,0:T(8,128)(2,1)S(1)}, u32[]{:S(2)}, u32[]{:S(2)}) collective-permute-start(bf16[63,1024]{1,0:T(8,128)(2,1)S(1)} %slice.20), channel_id=1, source_target_pairs={{0,8},{8,16},{16,24},{24,32},{32,40},{40,48},{48,56},{56,64},{64,7... | collective-permute-start | bytes 387080 | tf_op jit(solution)/shard_map/ppermute | solution.py:18
  199.1 0.1 slice.21
  199.2 1.8 collective-permute-done.1
  201.0 1.5 pad_maximum_fusion.1
  (10 shorter events, 0.1 us)
Async XLA Ops:
  6.5 18.0 %copy-start = (bf16[8,128,128]{2,1,0:T(8,128)(2,1)S(1)}, bf16[8,128,128]{2,1,0:T(8,128)(2,1)}, u32[]{:S(2)}) copy-start(bf16[8,128,128]{2,1,0:T(8,128)(2,1)} %param.9) | copy-start | bytes 786436
  27.1 4.5 %copy-start.3 = (s32[12,2]{0,1:T(2,128)S(1)}, s32[12,2]{0,1:T(2,128)}, u32[]{:S(2)}) copy-start(s32[12,2]{0,1:T(2,128)} %param.10) | copy-start | bytes 292
  27.1 32.9 %all-to-all-start.1 = ((bf16[32,2,128,128]{3,2,1,0:T(8,128)(2,1)}), bf16[32,2,128,128]{3,2,1,0:T(8,128)(2,1)S(1)}, u32[]{:S(2)}, u32[]{:S(2)}) async-start(bf16[32,2,128,128]{3,2,1,0:T(8,128)(2,1)} %broadcast_select_fusion), calls=%async_computation.1 | async-start | bytes 4194304 | tf_op jit(solution)/shard_map/all_to_all | solution.py:88
  31.5 103.6 %all-gather.2.cloned.1.call-start = ((), (), s32[]{:S(2)}) async-start(), calls=%async_computation.2 | async-start | bytes 7077888 | tf_op jit(solution)/shard_map/all_gather | solution.py:101
  60.7 1.7 copy-start.2
  62.4 6.3 %collective-permute-start = (bf16[63,1024]{1,0:T(8,128)(2,1)S(1)}, bf16[63,1024]{1,0:T(8,128)(2,1)S(1)}, u32[]{:S(2)}, u32[]{:S(2)}) collective-permute-start(bf16[63,1024]{1,0:T(8,128)(2,1)S(1)} %slice.13), channel_id=1, source_target_pairs={{8,0},{16,8},{24,16},{32,24},{40,32},{48,40},{56,48},{64,56},{72,6... | collective-permute-start | bytes 387080 | tf_op jit(solution)/shard_map/ppermute | solution.py:18
  135.1 1.6 copy-start.1
  195.2 5.8 %collective-permute-start.1 = (bf16[63,1024]{1,0:T(8,128)(2,1)S(1)}, bf16[63,1024]{1,0:T(8,128)(2,1)S(1)}, u32[]{:S(2)}, u32[]{:S(2)}) collective-permute-start(bf16[63,1024]{1,0:T(8,128)(2,1)S(1)} %slice.20), channel_id=1, source_target_pairs={{0,8},{8,16},{16,24},{24,32},{32,40},{40,48},{48,56},{56,64},{64,7... | collective-permute-start | bytes 387080 | tf_op jit(solution)/shard_map/ppermute | solution.py:18
Sparse Core Ops, SparseCore 0:
  61.8 73.2 all-gather.1
